TPU v7x, 128 devices: a whole 4x4x4 slice. The times are simulated.
128 devices in a mesh: pipe: 2 (over y_lo), tensor: 8 (over y_hi, x), dp: 8 (over z, core).
Axes of the slice: x: 4, y: 4 (y_hi: 2, y_lo: 2; y = y_hi * 2 + y_lo), z: 4, core: 2. Of those that a mesh axis runs over, the one named last changes fastest.
Arguments:
- section_input: bfloat16 [8192, 1024], P('dp'), may hold values from -6 to 6
- segment_ids: int32 [8192], P('dp'), may hold values from 0 to 127, never falling along the last dimension, each value on 1 to 256 neighbouring positions
- w_qkv: bfloat16 [2, 1024, 3, 1024], P('pipe', None, None, 'tensor'), may hold values from -0.1875 to 0.1875
- qv_bias: float32 [2, 2, 1024], P('pipe', None, 'tensor'), may hold values from -3 to 3
- w_out: bfloat16 [2, 1024, 1024], P('pipe', 'tensor'), may hold values from -0.75 to 0.75
- out_bias: float32 [2, 1024], P('pipe'), may hold values from -3 to 3
- w_up: bfloat16 [2, 1024, 4096], P('pipe', None, 'tensor'), may hold values from -0.1875 to 0.1875
- up_bias: float32 [2, 4096], P('pipe', 'tensor'), may hold values from -3 to 3
- w_down: bfloat16 [2, 4096, 1024], P('pipe', 'tensor'), may hold values from -0.09375 to 0.09375
- down_bias: float32 [2, 1024], P('pipe'), may hold values from -4 to 4
- norm_gains: float32 [2, 2, 1024], P('pipe'), may hold values from 0.25 to 1.75
- norm_shifts: float32 [2, 2, 1024], P('pipe'), may hold values from -2 to 2
- out_grad: bfloat16 [8192, 1024], P('dp'), may hold values from -6 to 6
Outputs:
- section_outputs: bfloat16 [2, 8192, 1024], P('pipe', 'dp')
- input_grads: bfloat16 [2, 8192, 1024], P('pipe', 'dp')
- grad_qkv: float32 [2, 1024, 3, 1024], P('pipe', None, None, 'tensor')
- grad_qv_bias: float32 [2, 2, 1024], P('pipe', None, 'tensor')
- grad_w_out: float32 [2, 1024, 1024], P('pipe', 'tensor')
- grad_out_bias: float32 [2, 1024], P('pipe')
- grad_w_up: float32 [2, 1024, 4096], P('pipe', None, 'tensor')
- grad_up_bias: float32 [2, 4096], P('pipe', 'tensor')
- grad_w_down: float32 [2, 4096, 1024], P('pipe', 'tensor')
- grad_down_bias: float32 [2, 1024], P('pipe')
- grad_gains: float32 [2, 2, 1024], P('pipe')
- grad_shifts: float32 [2, 2, 1024], P('pipe')
Inputs may be any that keep to these rules, and one draw needn't show every extreme that they name: `segment_ids`: ids never fall along the tokens; one document is 1 to 256 tokens.
All inputs are finite; a program needn't handle non-finite values.
Results may differ from a plain program's by a relative error of at most 0.035.
Values may be sent and summed in bfloat16 or wider, within the bound.
A program may use at most 128 MiB of HBM per device.

v0:
```python
import jax
import jax.numpy as jnp
from jax import lax
from jax.sharding import PartitionSpec as P

HEAD_DIM = 64
SEQ_LEN = 256
SEQ_MB = 1
NORM_EPS = 1e-05
GELU_COEF = 0.7978845608028654
CUBIC_COEF = 0.044715
MASKED_SCORE = -1e30


def passed_along(x, axis, by):
    peers = lax.axis_size(axis)
    pairs = [(i, i + by) for i in range(peers) if 0 <= i + by < peers]
    return lax.ppermute(x, axis, pairs)


def gelu_pair(pre_act):
    tanh_val = jnp.tanh(GELU_COEF * (pre_act + CUBIC_COEF * pre_act * pre_act * pre_act))
    gelu_value = 0.5 * pre_act * (1.0 + tanh_val)
    act_slope = 0.5 * (1.0 + tanh_val) + 0.5 * pre_act * (1.0 - tanh_val * tanh_val) * GELU_COEF * (
        1.0 + 3.0 * CUBIC_COEF * pre_act * pre_act
    )
    return (gelu_value, act_slope)


def layer_norm(rows_in, norm_gain, norm_shift):
    centred = rows_in - jnp.mean(rows_in, axis=-1, keepdims=True)
    inv_std = lax.rsqrt(jnp.mean(centred * centred, axis=-1, keepdims=True) + NORM_EPS)
    normed = centred * inv_std
    return (normed * norm_gain + norm_shift, normed, inv_std)


def norm_back(grad_out, normed, inv_std, norm_gain):
    scaled = grad_out * norm_gain
    return inv_std * (
        scaled
        - jnp.mean(scaled, axis=-1, keepdims=True)
        - normed * jnp.mean(scaled * normed, axis=-1, keepdims=True)
    )


def visible(seg_rows):
    length = seg_rows.shape[-1]
    position = jnp.arange(length)
    causal = position[:, None] >= position[None, :]
    same_doc = seg_rows[:, :, None] == seg_rows[:, None, :]
    return (causal[None] & same_doc)[:, None]


def scores_of(query_rows, key_rows, seg_rows):
    score_scale = query_rows.shape[-1] ** (-0.5)
    raw_scores = (
        jnp.einsum("sqhe,skhe->shqk", query_rows, key_rows, preferred_element_type=jnp.float32)
        * score_scale
    )
    return (jnp.where(visible(seg_rows), raw_scores, MASKED_SCORE), score_scale)


def attend(query_rows, key_rows, value_rows, seg_rows):
    scores, score_scale = scores_of(query_rows, key_rows, seg_rows)
    row_max = jnp.max(scores, axis=-1, keepdims=True)
    log_total = row_max + jnp.log(jnp.sum(jnp.exp(scores - row_max), axis=-1, keepdims=True))
    prob_rows = jnp.exp(scores - log_total).astype(jnp.bfloat16)
    mix_rows = jnp.einsum(
        "shqk,skhe->sqhe", prob_rows, value_rows, preferred_element_type=jnp.float32
    ).astype(jnp.bfloat16)
    return (mix_rows, log_total)


def attend_back(query_rows, key_rows, value_rows, seg_rows, log_total, grad_mix):
    scores, score_scale = scores_of(query_rows, key_rows, seg_rows)
    prob_rows = jnp.exp(scores - log_total)
    grad_prob = jnp.einsum(
        "sqhe,skhe->shqk", grad_mix, value_rows, preferred_element_type=jnp.float32
    )
    row_delta = jnp.sum(prob_rows * grad_prob, axis=-1, keepdims=True)
    grad_scores = (prob_rows * (grad_prob - row_delta) * score_scale).astype(jnp.bfloat16)
    g_query = jnp.einsum(
        "shqk,skhe->sqhe", grad_scores, key_rows, preferred_element_type=jnp.float32
    ).astype(jnp.bfloat16)
    g_key = jnp.einsum(
        "shqk,sqhe->skhe", grad_scores, query_rows, preferred_element_type=jnp.float32
    ).astype(jnp.bfloat16)
    g_value = jnp.einsum(
        "shqk,sqhe->skhe",
        prob_rows.astype(jnp.bfloat16),
        grad_mix,
        preferred_element_type=jnp.float32,
    ).astype(jnp.bfloat16)
    return (g_query, g_key, g_value)


def on_device(
    section_input,
    segment_ids,
    w_qkv,
    qv_bias,
    w_out,
    out_bias,
    w_up,
    up_bias,
    w_down,
    down_bias,
    norm_gains,
    norm_shifts,
    out_grad,
):
    section_index = lax.axis_index("pipe")
    is_first = section_index == 0
    proj_in = w_qkv[0]
    proj_out = w_out[0]
    up_proj = w_up[0]
    down_proj = w_down[0]
    out_shift = out_bias[0]
    up_shift = up_bias[0]
    down_shift = down_bias[0]
    norm_gain = norm_gains[0]
    norm_shift = norm_shifts[0]
    dmodel = proj_in.shape[0]
    columns = proj_in.shape[2]
    heads_here = columns // HEAD_DIM
    zero_row = jnp.zeros((1, columns), jnp.float32)
    qkv_shift = jnp.concatenate([qv_bias[0][0:1], zero_row, qv_bias[0][1:2]], axis=0)
    rows_mb = SEQ_MB * SEQ_LEN
    micro_count = section_input.shape[0] // rows_mb

    def combine(partial_rows):
        summed = lax.psum(partial_rows.astype(jnp.bfloat16), "tensor").astype(jnp.float32)
        return summed

    def batch_rows(source, batch_index):
        return lax.dynamic_slice_in_dim(source, batch_index * rows_mb, rows_mb, 0)

    incoming = jnp.zeros((rows_mb, dmodel), jnp.bfloat16)
    forward_outs = []
    states = []
    for tick_index in range(micro_count + 1):
        own_rows = batch_rows(section_input, min(tick_index, micro_count - 1))
        held_rows = jnp.where(is_first, own_rows, incoming)
        batch_here = jnp.clip(tick_index - section_index, 0, micro_count - 1)
        seg_rows = lax.dynamic_slice_in_dim(segment_ids, batch_here * rows_mb, rows_mb, 0).reshape(
            SEQ_MB, SEQ_LEN
        )
        residual = held_rows.astype(jnp.float32)
        first_norm, forward_normed1, forward_inv1 = layer_norm(
            residual, norm_gain[0], norm_shift[0]
        )
        forward_first_in = first_norm.astype(jnp.bfloat16)
        forward_qkv = (
            jnp.einsum("td,dgc->tgc", forward_first_in, proj_in, preferred_element_type=jnp.float32)
            + qkv_shift
        ).astype(jnp.bfloat16)
        forward_shaped = forward_qkv.reshape(SEQ_MB, SEQ_LEN, 3, heads_here, HEAD_DIM)
        mix_rows, forward_log_total = attend(
            forward_shaped[:, :, 0], forward_shaped[:, :, 1], forward_shaped[:, :, 2], seg_rows
        )
        forward_mix_flat = mix_rows.reshape(rows_mb, columns)
        middle = (
            residual
            + combine(jnp.dot(forward_mix_flat, proj_out, preferred_element_type=jnp.float32))
            + out_shift
        )
        second_norm, forward_normed2, forward_inv2 = layer_norm(middle, norm_gain[1], norm_shift[1])
        forward_second_in = second_norm.astype(jnp.bfloat16)
        pre_act = jnp.dot(forward_second_in, up_proj, preferred_element_type=jnp.float32) + up_shift
        gelu_value, forward_act_slope = gelu_pair(pre_act)
        forward_hidden = gelu_value.astype(jnp.bfloat16)
        result = (
            middle
            + combine(jnp.dot(forward_hidden, down_proj, preferred_element_type=jnp.float32))
            + down_shift
        ).astype(jnp.bfloat16)
        forward_kept_state = (
            forward_normed1,
            forward_inv1,
            forward_first_in,
            forward_qkv,
            forward_mix_flat,
            forward_log_total,
            forward_normed2,
            forward_inv2,
            forward_second_in,
            forward_act_slope,
            forward_hidden,
            seg_rows,
        )
        result, kept_state = (result, forward_kept_state)
        forward_outs.append(result)
        states.append(kept_state)
        incoming = passed_along(result, "pipe", 1)
    returning = jnp.zeros_like(incoming)
    back_outs = []
    grad_sums = None
    for tick_index in range(micro_count + 1):
        if tick_index < micro_count:
            own_grad = batch_rows(out_grad, micro_count - 1 - tick_index)
        else:
            own_grad = jnp.zeros_like(returning)
        cotangent = jnp.where(is_first, returning, own_grad)
        (
            normed1,
            inv1,
            first_in,
            qkv,
            mix_flat,
            log_total,
            normed2,
            inv2,
            second_in,
            act_slope,
            hidden,
            backward_seg_rows,
        ) = states[micro_count - tick_index]
        grad_top = cotangent.astype(jnp.float32)
        backward_g_down = jnp.einsum(
            "tf,td->fd", hidden, cotangent, preferred_element_type=jnp.float32
        )
        backward_g_down_shift = jnp.sum(grad_top, axis=0)
        g_hidden = jnp.einsum("td,fd->tf", cotangent, down_proj, preferred_element_type=jnp.float32)
        g_pre = (g_hidden * act_slope).astype(jnp.bfloat16)
        backward_g_up = jnp.einsum(
            "td,tf->df", second_in, g_pre, preferred_element_type=jnp.float32
        )
        backward_g_up_shift = jnp.sum(g_pre.astype(jnp.float32), axis=0)
        g_second = combine(
            jnp.einsum("tf,df->td", g_pre, up_proj, preferred_element_type=jnp.float32)
        )
        g_middle = grad_top + norm_back(g_second, normed2, inv2, norm_gain[1])
        g_gain2 = jnp.sum(g_second * normed2, axis=0)
        g_shift2 = jnp.sum(g_second, axis=0)
        middle_full = g_middle.astype(jnp.bfloat16)
        backward_g_proj_out = jnp.einsum(
            "tc,td->cd", mix_flat, middle_full, preferred_element_type=jnp.float32
        )
        backward_g_out_shift = jnp.sum(g_middle, axis=0)
        g_mix = jnp.einsum(
            "td,cd->tc", middle_full, proj_out, preferred_element_type=jnp.float32
        ).astype(jnp.bfloat16)
        shaped = qkv.reshape(SEQ_MB, SEQ_LEN, 3, heads_here, HEAD_DIM)
        g_query, g_key, g_value = attend_back(
            shaped[:, :, 0],
            shaped[:, :, 1],
            shaped[:, :, 2],
            backward_seg_rows,
            log_total,
            g_mix.reshape(SEQ_MB, SEQ_LEN, heads_here, HEAD_DIM),
        )
        g_qkv = jnp.stack([g_query, g_key, g_value], axis=2).reshape(rows_mb, 3, columns)
        backward_g_proj_in = jnp.einsum(
            "td,tgc->dgc", first_in, g_qkv, preferred_element_type=jnp.float32
        )
        qkv_sums = jnp.sum(g_qkv.astype(jnp.float32), axis=0)
        backward_g_qv = jnp.stack([qkv_sums[0], qkv_sums[2]], axis=0)
        g_first = combine(
            jnp.einsum("tgc,dgc->td", g_qkv, proj_in, preferred_element_type=jnp.float32)
        )
        g_gain1 = jnp.sum(g_first * normed1, axis=0)
        g_shift1 = jnp.sum(g_first, axis=0)
        g_low = (g_middle + norm_back(g_first, normed1, inv1, norm_gain[0])).astype(jnp.bfloat16)
        grads = (
            backward_g_proj_in,
            backward_g_qv,
            backward_g_proj_out,
            backward_g_out_shift,
            backward_g_up,
            backward_g_up_shift,
            backward_g_down,
            backward_g_down_shift,
            jnp.stack([g_gain1, g_gain2]),
            jnp.stack([g_shift1, g_shift2]),
        )
        g_low, grads = (g_low, grads)
        grad_sums = (
            grads
            if grad_sums is None
            else tuple((held + fresh for held, fresh in zip(grad_sums, grads)))
        )
        back_outs.append(g_low)
        returning = passed_along(g_low, "pipe", -1)
    out_list = [
        jnp.where(is_first, forward_outs[batch_index], forward_outs[batch_index + 1])
        for batch_index in range(micro_count)
    ]
    in_list = [
        jnp.where(
            is_first, back_outs[micro_count - batch_index], back_outs[micro_count - 1 - batch_index]
        )
        for batch_index in range(micro_count)
    ]
    (
        g_proj_in,
        g_qv,
        g_proj_out,
        g_out_shift,
        g_up,
        g_up_shift,
        g_down,
        g_down_shift,
        g_gains,
        g_shifts,
    ) = grad_sums
    out_full = jnp.concatenate(out_list, axis=0)
    in_full = jnp.concatenate(in_list, axis=0)
    (
        total_qkv,
        total_qv,
        total_out,
        total_up,
        total_up_shift,
        total_down,
        total_out_shift,
        total_down_shift,
        total_gains,
        total_shifts,
    ) = (
        lax.psum(g_proj_in.astype(jnp.bfloat16), "dp").astype(jnp.float32),
        lax.psum(g_qv.astype(jnp.bfloat16), "dp").astype(jnp.float32),
        lax.psum(g_proj_out.astype(jnp.bfloat16), "dp").astype(jnp.float32),
        lax.psum(g_up.astype(jnp.bfloat16), "dp").astype(jnp.float32),
        lax.psum(g_up_shift.astype(jnp.bfloat16), "dp").astype(jnp.float32),
        lax.psum(g_down.astype(jnp.bfloat16), "dp").astype(jnp.float32),
        lax.psum(g_out_shift.astype(jnp.bfloat16), "dp").astype(jnp.float32),
        lax.psum(g_down_shift.astype(jnp.bfloat16), "dp").astype(jnp.float32),
        lax.psum(g_gains.astype(jnp.bfloat16), "dp").astype(jnp.float32),
        lax.psum(g_shifts.astype(jnp.bfloat16), "dp").astype(jnp.float32),
    )
    return (
        out_full[None],
        in_full[None],
        total_qkv[None],
        total_qv[None],
        total_out[None],
        total_out_shift[None],
        total_up[None],
        total_up_shift[None],
        total_down[None],
        total_down_shift[None],
        total_gains[None],
        total_shifts[None],
    )


def solution(mesh):
    placed = (
        P("dp", None),
        P("dp"),
        P("pipe", None, None, "tensor"),
        P("pipe", None, "tensor"),
        P("pipe", "tensor", None),
        P("pipe", None),
        P("pipe", None, "tensor"),
        P("pipe", "tensor"),
        P("pipe", "tensor", None),
        P("pipe", None),
        P("pipe", None, None),
        P("pipe", None, None),
        P("dp", None),
    )
    return jax.shard_map(
        on_device,
        mesh=mesh,
        in_specs=placed,
        out_specs=(
            P("pipe", "dp", None),
            P("pipe", "dp", None),
            P("pipe", None, None, "tensor"),
            P("pipe", None, "tensor"),
            P("pipe", "tensor", None),
            P("pipe", None),
            P("pipe", None, "tensor"),
            P("pipe", "tensor"),
            P("pipe", "tensor", None),
            P("pipe", None),
            P("pipe", None, None),
            P("pipe", None, None),
        ),
        check_vma=False,
    )
```

profile of v0, /device:TPU:0, one launch (start us, length us, event | category | flops | bytes accessed | tf_op | source)
XLA Modules:
  0.0 1970.8 jit_solution(4981071526094199700)
XLA Ops:
  17.0 87.8 %all-reduce.24.cloned.1.call-done = bf16[256,1024]{1,0:T(8,128)(2,1)} async-done(((bf16[256,1024]{1,0:T(8,128)(2,1)}), bf16[256,1024]{1,0:T(8,128)(2,1)}) %all-reduce.24.cloned.1.call-update) | async-done | bytes 524304 | tf_op jit(solution)/shard_map/psum | solution.py:132
  111.8 83.5 %all-reduce.26.cloned.1.call-done = bf16[256,1024]{1,0:T(8,128)(2,1)} async-done(((bf16[256,1024]{1,0:T(8,128)(2,1)}), bf16[256,1024]{1,0:T(8,128)(2,1)}) %all-reduce.26.cloned.1.call-update) | async-done | bytes 524304 | tf_op jit(solution)/shard_map/psum | solution.py:132
  199.5 6.5 collective-permute-done
  211.0 85.1 %all-reduce.28.cloned.1.call-done = bf16[256,1024]{1,0:T(8,128)(2,1)} async-done(((bf16[256,1024]{1,0:T(8,128)(2,1)}), bf16[256,1024]{1,0:T(8,128)(2,1)}) %all-reduce.28.cloned.1.call-update) | async-done | bytes 524304 | tf_op jit(solution)/shard_map/psum | solution.py:132
  301.6 83.4 %all-reduce.30.cloned.1.call-done = bf16[256,1024]{1,0:T(8,128)(2,1)} async-done(((bf16[256,1024]{1,0:T(8,128)(2,1)}), bf16[256,1024]{1,0:T(8,128)(2,1)}) %all-reduce.30.cloned.1.call-update) | async-done | bytes 524304 | tf_op jit(solution)/shard_map/psum | solution.py:132
  390.0 6.5 collective-permute-done.1
  401.5 85.1 %all-reduce.32.cloned.1.call-done = bf16[256,1024]{1,0:T(8,128)(2,1)} async-done(((bf16[256,1024]{1,0:T(8,128)(2,1)}), bf16[256,1024]{1,0:T(8,128)(2,1)}) %all-reduce.32.cloned.1.call-update) | async-done | bytes 524304 | tf_op jit(solution)/shard_map/psum | solution.py:132
  493.3 83.4 %all-reduce.34.cloned.1.call-done = bf16[256,1024]{1,0:T(8,128)(2,1)} async-done(((bf16[256,1024]{1,0:T(8,128)(2,1)}), bf16[256,1024]{1,0:T(8,128)(2,1)}) %all-reduce.34.cloned.1.call-update) | async-done | bytes 524304 | tf_op jit(solution)/shard_map/psum | solution.py:132
  581.9 6.4 collective-permute-done.2
  593.3 85.1 %all-reduce.36.cloned.1.call-done = bf16[256,1024]{1,0:T(8,128)(2,1)} async-done(((bf16[256,1024]{1,0:T(8,128)(2,1)}), bf16[256,1024]{1,0:T(8,128)(2,1)}) %all-reduce.36.cloned.1.call-update) | async-done | bytes 524304 | tf_op jit(solution)/shard_map/psum | solution.py:132
  683.9 83.5 %all-reduce.38.cloned.1.call-done = bf16[256,1024]{1,0:T(8,128)(2,1)} async-done(((bf16[256,1024]{1,0:T(8,128)(2,1)}), bf16[256,1024]{1,0:T(8,128)(2,1)}) %all-reduce.38.cloned.1.call-update) | async-done | bytes 524304 | tf_op jit(solution)/shard_map/psum | solution.py:132
  772.3 6.5 collective-permute-done.3
  784.3 85.1 %all-reduce.40.cloned.1.call-done = bf16[256,1024]{1,0:T(8,128)(2,1)} async-done(((bf16[256,1024]{1,0:T(8,128)(2,1)}), bf16[256,1024]{1,0:T(8,128)(2,1)}) %all-reduce.40.cloned.1.call-update) | async-done | bytes 524304 | tf_op jit(solution)/shard_map/psum | solution.py:132
  877.3 83.4 %all-reduce.42.cloned.1.call-done = bf16[256,1024]{1,0:T(8,128)(2,1)} async-done(((bf16[256,1024]{1,0:T(8,128)(2,1)}), bf16[256,1024]{1,0:T(8,128)(2,1)}) %all-reduce.42.cloned.1.call-update) | async-done | bytes 524304 | tf_op jit(solution)/shard_map/psum | solution.py:132
  980.4 83.5 %all-reduce.44.cloned.1.call-done = bf16[256,1024]{1,0:T(8,128)(2,1)} async-done(((bf16[256,1024]{1,0:T(8,128)(2,1)}), bf16[256,1024]{1,0:T(8,128)(2,1)}) %all-reduce.44.cloned.1.call-update) | async-done | bytes 524304 | tf_op jit(solution)/shard_map/psum | solution.py:132
  1071.8 7.6 collective-permute-done.4
  1083.6 3.2 fusion.314
  1088.7 78.3 %all-reduce.46.cloned.1.call-done = bf16[256,1024]{1,0:T(8,128)(2,1)} async-done(((bf16[256,1024]{1,0:T(8,128)(2,1)}), bf16[256,1024]{1,0:T(8,128)(2,1)}) %all-reduce.46.cloned.1.call-update) | async-done | bytes 524304 | tf_op jit(solution)/shard_map/psum | solution.py:132
  1195.3 78.5 %all-reduce.48.cloned.1.call-done = bf16[256,1024]{1,0:T(8,128)(2,1)} async-done(((bf16[256,1024]{1,0:T(8,128)(2,1)}), bf16[256,1024]{1,0:T(8,128)(2,1)}) %all-reduce.48.cloned.1.call-update) | async-done | bytes 524304 | tf_op jit(solution)/shard_map/psum | solution.py:132
  1284.7 5.3 collective-permute-done.5
  1299.4 79.2 %all-reduce.50.cloned.1.call-done = bf16[256,1024]{1,0:T(8,128)(2,1)} async-done(((bf16[256,1024]{1,0:T(8,128)(2,1)}), bf16[256,1024]{1,0:T(8,128)(2,1)}) %all-reduce.50.cloned.1.call-update) | async-done | bytes 524304 | tf_op jit(solution)/shard_map/psum | solution.py:132
  1402.1 79.1 %all-reduce.52.cloned.1.call-done = bf16[256,1024]{1,0:T(8,128)(2,1)} async-done(((bf16[256,1024]{1,0:T(8,128)(2,1)}), bf16[256,1024]{1,0:T(8,128)(2,1)}) %all-reduce.52.cloned.1.call-update) | async-done | bytes 524304 | tf_op jit(solution)/shard_map/psum | solution.py:132
  1492.0 5.4 collective-permute-done.6
  1506.0 80.1 %all-reduce.54.cloned.1.call-done = bf16[256,1024]{1,0:T(8,128)(2,1)} async-done(((bf16[256,1024]{1,0:T(8,128)(2,1)}), bf16[256,1024]{1,0:T(8,128)(2,1)}) %all-reduce.54.cloned.1.call-update) | async-done | bytes 524304 | tf_op jit(solution)/shard_map/psum | solution.py:132
  1604.0 79.6 %all-reduce.56.cloned.1.call-done = bf16[256,1024]{1,0:T(8,128)(2,1)} async-done(((bf16[256,1024]{1,0:T(8,128)(2,1)}), bf16[256,1024]{1,0:T(8,128)(2,1)}) %all-reduce.56.cloned.1.call-update) | async-done | bytes 524304 | tf_op jit(solution)/shard_map/psum | solution.py:132
  1692.8 7.0 collective-permute-done.7
  1702.7 5.6 fusion.166
  1712.4 73.1 %all-reduce.58.cloned.1.call-done = bf16[256,1024]{1,0:T(8,128)(2,1)} async-done(((bf16[256,1024]{1,0:T(8,128)(2,1)}), bf16[256,1024]{1,0:T(8,128)(2,1)}) %all-reduce.58.cloned.1.call-update) | async-done | bytes 524304 | tf_op jit(solution)/shard_map/psum | solution.py:132
  1804.3 3.8 fusion.36
  1808.9 77.5 %all-reduce.62.cloned.1.call-done = (bf16[256,1024]{1,0:T(8,128)(2,1)}, bf16[256,1024]{1,0:T(8,128)(2,1)}) async-done(((bf16[256,1024]{1,0:T(8,128)(2,1)}, bf16[256,1024]{1,0:T(8,128)(2,1)}), (bf16[256,1024]{1,0:T(8,128)(2,1)}, bf16[256,1024]{1,0:T(8,128)(2,1)})) %all-reduce.62.cloned.1.call-update) | async-done | bytes 1048592 | tf_op jit(solution)/shard_map/psum | solution.py:132
  1888.5 24.1 %all-reduce = (bf16[1,2,128]{2,1,0:T(2,128)(2,1)S(1)}, bf16[1,1024]{1,0:T(2,128)(2,1)S(1)}, bf16[1,512]{1,0:T(2,128)(2,1)S(1)}, bf16[1,1024]{1,0:T(2,128)(2,1)S(...) all-reduce(bf16[1,2,128]{2,1,0:T(2,128)(2,1)S(1)} %fusion.354, ...), channel_id=1, replica_groups=mesh['pipe'=2,'tensor'=8,'dp'=8] {'dp'}, use_global_device_ids=true, to_apply=%region_81.82 | all-reduce | flops 6912 | bytes 27648 | tf_op jit(solution)/shard_map/psum | solution.py:321
  1922.3 34.8 %all-reduce.60.cloned.1.call-done = (bf16[1,1024,3,128]{3,1,2,0:T(8,128)(2,1)}, bf16[1,128,1024]{2,1,0:T(8,128)(2,1)}, bf16[1,1024,512]{2,1,0:T(8,128)(2,1)}, bf16[1,512,1024]{2,1,0:T(8,128)(2,1)}) async-done(((bf16[1,1024,3,128]{3,1,2,0:T(8,128)(2,1)}, bf16[1,128,1024]{2,1,0:T(8,128)(2,1)}, bf16[1,1024,512]{2,1,0:T(8,128)(2,1)}, bf16[1,512,1024]{2,1,0:T(8,128)(2,1)}), (bf16[1,1024,3,128]{3,1,2,0:T(8,128)(2,1)}, ...) | async-done | bytes 3145744 | tf_op jit(solution)/shard_map/psum | solution.py:320
  (696 shorter events, 277.1 us)
Async XLA Ops:
  7.2 97.6 %all-reduce.24.cloned.1.call-start = ((), (), s32[]{:S(2)}) async-start(), calls=%async_computation | async-start | bytes 1048576 | tf_op jit(solution)/shard_map/psum | solution.py:132
  11.5 768.9 %copy-start.146 = (f32[1,1,1024]{2,1,0:T(1,128)}, f32[1,1,1024]{2,1,0:T(1,128)S(1)}, u32[]{:S(2)}) copy-start(f32[1,1,1024]{2,1,0:T(1,128)S(1)} %get-tuple-element.104) | copy-start | bytes 12292
  16.9 178.3 %all-reduce.26.cloned.1.call-start = ((), (), s32[]{:S(2)}) async-start(), calls=%async_computation.1 | async-start | bytes 1048576 | tf_op jit(solution)/shard_map/psum | solution.py:132
  111.7 184.3 %all-reduce.28.cloned.1.call-start = ((), (), s32[]{:S(2)}) async-start(), calls=%async_computation.2 | async-start | bytes 1048576 | tf_op jit(solution)/shard_map/psum | solution.py:132
  196.8 9.2 collective-permute-start
  210.9 174.0 %all-reduce.30.cloned.1.call-start = ((), (), s32[]{:S(2)}) async-start(), calls=%async_computation.3 | async-start | bytes 1048576 | tf_op jit(solution)/shard_map/psum | solution.py:132
  301.5 185.1 %all-reduce.32.cloned.1.call-start = ((), (), s32[]{:S(2)}) async-start(), calls=%async_computation.4 | async-start | bytes 1048576 | tf_op jit(solution)/shard_map/psum | solution.py:132
  387.3 9.2 collective-permute-start.1
  401.4 175.3 %all-reduce.34.cloned.1.call-start = ((), (), s32[]{:S(2)}) async-start(), calls=%async_computation.5 | async-start | bytes 1048576 | tf_op jit(solution)/shard_map/psum | solution.py:132
  493.3 185.0 %all-reduce.36.cloned.1.call-start = ((), (), s32[]{:S(2)}) async-start(), calls=%async_computation.6 | async-start | bytes 1048576 | tf_op jit(solution)/shard_map/psum | solution.py:132
  579.1 9.2 collective-permute-start.2
  593.2 174.2 %all-reduce.38.cloned.1.call-start = ((), (), s32[]{:S(2)}) async-start(), calls=%async_computation.7 | async-start | bytes 1048576 | tf_op jit(solution)/shard_map/psum | solution.py:132
  683.8 185.6 %all-reduce.40.cloned.1.call-start = ((), (), s32[]{:S(2)}) async-start(), calls=%async_computation.8 | async-start | bytes 1048576 | tf_op jit(solution)/shard_map/psum | solution.py:132
  769.8 9.0 collective-permute-start.3
  784.2 176.5 %all-reduce.42.cloned.1.call-start = ((), (), s32[]{:S(2)}) async-start(), calls=%async_computation.9 | async-start | bytes 1048576 | tf_op jit(solution)/shard_map/psum | solution.py:132
  877.2 186.6 %all-reduce.44.cloned.1.call-start = ((), (), s32[]{:S(2)}) async-start(), calls=%async_computation.10 | async-start | bytes 1048576 | tf_op jit(solution)/shard_map/psum | solution.py:132
  980.3 186.7 %all-reduce.46.cloned.1.call-start = ((), (), s32[]{:S(2)}) async-start(), calls=%async_computation.11 | async-start | bytes 1048576 | tf_op jit(solution)/shard_map/psum | solution.py:132
  1068.0 11.3 collective-permute-start.4
  1083.5 190.2 %all-reduce.48.cloned.1.call-start = ((), (), s32[]{:S(2)}) async-start(), calls=%async_computation.12 | async-start | bytes 1048576 | tf_op jit(solution)/shard_map/psum | solution.py:132
  1190.2 188.5 %all-reduce.50.cloned.1.call-start = ((), (), s32[]{:S(2)}) async-start(), calls=%async_computation.13 | async-start | bytes 1048576 | tf_op jit(solution)/shard_map/psum | solution.py:132
  1278.8 11.2 collective-permute-start.5
  1295.1 186.1 %all-reduce.52.cloned.1.call-start = ((), (), s32[]{:S(2)}) async-start(), calls=%async_computation.14 | async-start | bytes 1048576 | tf_op jit(solution)/shard_map/psum | solution.py:132
  1397.7 188.4 %all-reduce.54.cloned.1.call-start = ((), (), s32[]{:S(2)}) async-start(), calls=%async_computation.15 | async-start | bytes 1048576 | tf_op jit(solution)/shard_map/psum | solution.py:132
  1486.2 11.2 collective-permute-start.6
  1502.5 181.1 %all-reduce.56.cloned.1.call-start = ((), (), s32[]{:S(2)}) async-start(), calls=%async_computation.16 | async-start | bytes 1048576 | tf_op jit(solution)/shard_map/psum | solution.py:132
  1600.1 185.4 %all-reduce.58.cloned.1.call-start = ((), (), s32[]{:S(2)}) async-start(), calls=%async_computation.17 | async-start | bytes 1048576 | tf_op jit(solution)/shard_map/psum | solution.py:132
  1688.6 11.2 collective-permute-start.7
  1702.0 184.5 %all-reduce.62.cloned.1.call-start = ((), (), s32[]{:S(2)}) async-start(), calls=%async_computation.19 | async-start | bytes 2097152 | tf_op jit(solution)/shard_map/psum | solution.py:132
  1800.6 156.5 %all-reduce.60.cloned.1.call-start = ((), (), s32[]{:S(2)}) async-start(), calls=%async_computation.18 | async-start | bytes 6291456 | tf_op jit(solution)/shard_map/psum | solution.py:320
  1808.4 107.7 %copy-start.13 = (bf16[256,1024]{1,0:T(8,128)(2,1)S(1)}, bf16[256,1024]{1,0:T(8,128)(2,1)}, u32[]{:S(2)}) copy-start(bf16[256,1024]{1,0:T(8,128)(2,1)} %all-reduce.40.cloned.1.call-done) | copy-start | bytes 1572868
  1808.4 107.7 %copy-start.30 = (f32[256,1024]{1,0:T(8,128)S(1)}, f32[256,1024]{1,0:T(8,128)}, u32[]{:S(2)}) copy-start(f32[256,1024]{1,0:T(8,128)} %copy-done.29) | copy-start | bytes 3145732
  1808.4 107.7 %copy-start.117 = (f32[1,1024]{1,0:T(1,128)S(1)}, f32[1,1024]{1,0:T(1,128)}, u32[]{:S(2)}) copy-start(f32[1,1024]{1,0:T(1,128)} %param.22) | copy-start | bytes 12292
  (197 other events, 3920.5 us)
Sparse Core Ops, SparseCore 0:
  17.0 87.7 all-reduce.23
  111.9 83.3 all-reduce.25
  211.1 84.9 all-reduce.27
  301.6 83.3 all-reduce.29
  401.5 85.0 all-reduce.31
  493.4 83.2 all-reduce.33
  593.3 84.9 all-reduce.35
  683.9 83.3 all-reduce.37
  784.4 84.9 all-reduce.39
  877.4 83.2 all-reduce.41
  980.4 83.3 all-reduce.43
  1083.7 83.3 all-reduce.45
  1190.3 83.3 all-reduce.47
  1295.3 83.3 all-reduce.49
  1397.8 83.3 all-reduce.51
  1502.6 83.3 all-reduce.53
  1600.2 83.2 all-reduce.55
  1702.1 83.3 all-reduce.57
  1800.7 85.7 all-reduce.61
  1889.5 67.5 all-reduce.59
where the time goes:
time: 1980 us; the launch traced here: 1970 us
  waiting for transfers between devices  1640 us (83%)
  matrix products  134 us (7%)
  other arithmetic  103 us (5%)
  local copies, waits for them, and re-layouts  35.6 us (2%)
  blocking collectives  24.1 us (1%)
    psum x19, waiting for transfers between devices, combine(): lax.psum(partial_rows.astype(jnp.bfloat16), 'tensor').astype(jnp.float32)  1550 us
    ppermute x8, waiting for transfers between devices, passed_along(): return lax.ppermute(x, axis, pairs)  51.2 us
  transfers between devices with their start and end apart: 28, of which 28 were waited for; matrix products, arithmetic and copies ran while one was open for 3% of the time, Pallas kernels for 0%

commit v1 on v0

--- a/solution.py
+++ b/solution.py
@@ -129,7 +129,9 @@
     micro_count = section_input.shape[0] // rows_mb
 
     def combine(partial_rows):
-        summed = lax.psum(partial_rows.astype(jnp.bfloat16), "tensor").astype(jnp.float32)
+        summed = jnp.sum(
+            lax.all_gather(partial_rows.astype(jnp.bfloat16), "tensor"), axis=0
+        ).astype(jnp.float32)
         return summed
 
     def batch_rows(source, batch_index):

time: 1980 us -> 1910 us (0.965)
  waiting for transfers between devices: 1640 us -> 1510 us
  other arithmetic: 103 us -> 167 us
    psum x19 -> x0, waiting for transfers between devices: 1550 us -> none  [combine(): lax.psum(partial_rows.astype(jnp.bfloat16), 'tensor').astype(jnp.float32)]
    all_gather x0 -> x20, waiting for transfers between devices: none -> 1340 us  [combine(): lax.all_gather(partial_rows.astype(jnp.bfloat16), 'tensor')]
    reduce_sum x0 -> x20, other arithmetic: none -> 73.1 us  [combine(): jnp.sum(lax.all_gather(partial_rows.astype(jnp.bfloat16), 'tensor'), axis=0)]
    ppermute x8, waiting for transfers between devices: 51.2 us -> 98.2 us  [passed_along(): return lax.ppermute(x, axis, pairs)]
    psum x1, waiting for transfers between devices: 34.8 us -> 64.2 us  [on_device(): lax.psum(g_proj_in.astype(jnp.bfloat16), 'dp').astype(jnp.float32)]
  transfers between devices with their start and end apart: 28 -> 29, of which waited for: 28 -> 29; matrix products, arithmetic and copies ran while one was open for 3% -> 3% of each run, Pallas kernels for 0% -> 0%
where the time goes in v1:
time: 1910 us; the launch traced here: 1900 us
  waiting for transfers between devices  1510 us (79%)
  other arithmetic  167 us (9%)
  matrix products  123 us (6%)
  local copies, waits for them, and re-layouts  44.9 us (2%)
  blocking collectives  25.4 us (1%)
    all_gather x20, waiting for transfers between devices, combine(): lax.all_gather(partial_rows.astype(jnp.bfloat16), 'tensor')  1340 us
    ppermute x8, waiting for transfers between devices, passed_along(): return lax.ppermute(x, axis, pairs)  98.2 us
    reduce_sum x20, other arithmetic, combine(): jnp.sum(lax.all_gather(partial_rows.astype(jnp.bfloat16), 'tensor'), axis=0)  73.1 us
    psum x1, waiting for transfers between devices, on_device(): lax.psum(g_proj_in.astype(jnp.bfloat16), 'dp').astype(jnp.float32)  64.2 us
  transfers between devices with their start and end apart: 29, of which 29 were waited for; matrix products, arithmetic and copies ran while one was open for 3% of the time, Pallas kernels for 0%

profile of v1, /device:TPU:0, one launch (start us, length us, event | category | flops | bytes accessed | tf_op | source)
XLA Modules:
  0.0 1899.8 jit_solution(6527015564550638090)
XLA Ops:
  16.9 74.1 %all-gather.41.cloned.1.call-done = bf16[2048,1024]{1,0:T(8,128)(2,1)} async-done(((bf16[256,1024]{1,0:T(8,128)(2,1)}), bf16[2048,1024]{1,0:T(8,128)(2,1)}) %all-gather.41.cloned.1.call-update) | async-done | bytes 4194320 | tf_op jit(solution)/shard_map/all_gather | solution.py:133
  100.2 69.5 %all-gather.43.cloned.1.call-done = bf16[2048,1024]{1,0:T(8,128)(2,1)} async-done(((bf16[256,1024]{1,0:T(8,128)(2,1)}), bf16[2048,1024]{1,0:T(8,128)(2,1)}) %all-gather.43.cloned.1.call-update) | async-done | bytes 4194320 | tf_op jit(solution)/shard_map/all_gather | solution.py:133
  177.0 10.6 collective-permute-done
  192.6 71.4 %all-gather.45.cloned.1.call-done = bf16[2048,1024]{1,0:T(8,128)(2,1)} async-done(((bf16[256,1024]{1,0:T(8,128)(2,1)}), bf16[2048,1024]{1,0:T(8,128)(2,1)}) %all-gather.45.cloned.1.call-update) | async-done | bytes 4194320 | tf_op jit(solution)/shard_map/all_gather | solution.py:133
  270.6 69.4 %all-gather.47.cloned.1.call-done = bf16[2048,1024]{1,0:T(8,128)(2,1)} async-done(((bf16[256,1024]{1,0:T(8,128)(2,1)}), bf16[2048,1024]{1,0:T(8,128)(2,1)}) %all-gather.47.cloned.1.call-update) | async-done | bytes 4194320 | tf_op jit(solution)/shard_map/all_gather | solution.py:133
  348.8 10.7 collective-permute-done.1
  365.0 71.4 %all-gather.49.cloned.1.call-done = bf16[2048,1024]{1,0:T(8,128)(2,1)} async-done(((bf16[256,1024]{1,0:T(8,128)(2,1)}), bf16[2048,1024]{1,0:T(8,128)(2,1)}) %all-gather.49.cloned.1.call-update) | async-done | bytes 4194320 | tf_op jit(solution)/shard_map/all_gather | solution.py:133
  436.4 4.0 reduce_sum.1067
  446.0 69.6 %all-gather.51.cloned.1.call-done = bf16[2048,1024]{1,0:T(8,128)(2,1)} async-done(((bf16[256,1024]{1,0:T(8,128)(2,1)}), bf16[2048,1024]{1,0:T(8,128)(2,1)}) %all-gather.51.cloned.1.call-update) | async-done | bytes 4194320 | tf_op jit(solution)/shard_map/all_gather | solution.py:133
  522.6 10.8 collective-permute-done.2
  538.8 71.3 %all-gather.53.cloned.1.call-done = bf16[2048,1024]{1,0:T(8,128)(2,1)} async-done(((bf16[256,1024]{1,0:T(8,128)(2,1)}), bf16[2048,1024]{1,0:T(8,128)(2,1)}) %all-gather.53.cloned.1.call-update) | async-done | bytes 4194320 | tf_op jit(solution)/shard_map/all_gather | solution.py:133
  617.5 69.3 %all-gather.55.cloned.1.call-done = bf16[2048,1024]{1,0:T(8,128)(2,1)} async-done(((bf16[256,1024]{1,0:T(8,128)(2,1)}), bf16[2048,1024]{1,0:T(8,128)(2,1)}) %all-gather.55.cloned.1.call-update) | async-done | bytes 4194320 | tf_op jit(solution)/shard_map/all_gather | solution.py:133
  686.9 4.0 reduce_sum.1077
  695.7 10.7 collective-permute-done.3
  711.9 71.4 %all-gather.57.cloned.1.call-done = bf16[2048,1024]{1,0:T(8,128)(2,1)} async-done(((bf16[256,1024]{1,0:T(8,128)(2,1)}), bf16[2048,1024]{1,0:T(8,128)(2,1)}) %all-gather.57.cloned.1.call-update) | async-done | bytes 4194320 | tf_op jit(solution)/shard_map/all_gather | solution.py:133
  795.2 69.5 %all-gather.61.cloned.1.call-done = bf16[2048,1024]{1,0:T(8,128)(2,1)} async-done(((bf16[256,1024]{1,0:T(8,128)(2,1)}), bf16[2048,1024]{1,0:T(8,128)(2,1)}) %all-gather.61.cloned.1.call-update) | async-done | bytes 4194320 | tf_op jit(solution)/shard_map/all_gather | solution.py:133
  889.0 69.1 %all-gather.63.cloned.1.call-done = bf16[2048,1024]{1,0:T(8,128)(2,1)} async-done(((bf16[256,1024]{1,0:T(8,128)(2,1)}), bf16[2048,1024]{1,0:T(8,128)(2,1)}) %all-gather.63.cloned.1.call-update) | async-done | bytes 4194320 | tf_op jit(solution)/shard_map/all_gather | solution.py:133
  967.6 13.9 collective-permute-done.4
  985.7 69.0 %all-gather.65.cloned.1.call-done = bf16[2048,1024]{1,0:T(8,128)(2,1)} async-done(((bf16[256,1024]{1,0:T(8,128)(2,1)}), bf16[2048,1024]{1,0:T(8,128)(2,1)}) %all-gather.65.cloned.1.call-update) | async-done | bytes 4194320 | tf_op jit(solution)/shard_map/all_gather | solution.py:133
  1081.8 69.6 %all-gather.67.cloned.1.call-done = bf16[2048,1024]{1,0:T(8,128)(2,1)} async-done(((bf16[256,1024]{1,0:T(8,128)(2,1)}), bf16[2048,1024]{1,0:T(8,128)(2,1)}) %all-gather.67.cloned.1.call-update) | async-done | bytes 4194320 | tf_op jit(solution)/shard_map/all_gather | solution.py:133
  1161.7 13.9 collective-permute-done.5
  1180.8 68.8 %all-gather.69.cloned.1.call-done = bf16[2048,1024]{1,0:T(8,128)(2,1)} async-done(((bf16[256,1024]{1,0:T(8,128)(2,1)}), bf16[2048,1024]{1,0:T(8,128)(2,1)}) %all-gather.69.cloned.1.call-update) | async-done | bytes 4194320 | tf_op jit(solution)/shard_map/all_gather | solution.py:133
  1276.9 69.5 %all-gather.71.cloned.1.call-done = bf16[2048,1024]{1,0:T(8,128)(2,1)} async-done(((bf16[256,1024]{1,0:T(8,128)(2,1)}), bf16[2048,1024]{1,0:T(8,128)(2,1)}) %all-gather.71.cloned.1.call-update) | async-done | bytes 4194320 | tf_op jit(solution)/shard_map/all_gather | solution.py:133
  1356.7 13.9 collective-permute-done.6
  1375.7 69.0 %all-gather.73.cloned.1.call-done = bf16[2048,1024]{1,0:T(8,128)(2,1)} async-done(((bf16[256,1024]{1,0:T(8,128)(2,1)}), bf16[2048,1024]{1,0:T(8,128)(2,1)}) %all-gather.73.cloned.1.call-update) | async-done | bytes 4194320 | tf_op jit(solution)/shard_map/all_gather | solution.py:133
  1471.8 69.6 %all-gather.75.cloned.1.call-done = bf16[2048,1024]{1,0:T(8,128)(2,1)} async-done(((bf16[256,1024]{1,0:T(8,128)(2,1)}), bf16[2048,1024]{1,0:T(8,128)(2,1)}) %all-gather.75.cloned.1.call-update) | async-done | bytes 4194320 | tf_op jit(solution)/shard_map/all_gather | solution.py:133
  1551.7 13.9 collective-permute-done.7
  1598.4 39.5 %all-gather.77.cloned.1.call-done = bf16[2048,1024]{1,0:T(8,128)(2,1)} async-done(((bf16[256,1024]{1,0:T(8,128)(2,1)}), bf16[2048,1024]{1,0:T(8,128)(2,1)}) %all-gather.77.cloned.1.call-update) | async-done | bytes 4194320 | tf_op jit(solution)/shard_map/all_gather | solution.py:133
  1665.7 44.0 %all-gather.59.cloned.1.call-done = bf16[2048,1024]{1,0:T(8,128)(2,1)} async-done(((bf16[256,1024]{1,0:T(8,128)(2,1)}), bf16[2048,1024]{1,0:T(8,128)(2,1)}) %all-gather.59.cloned.1.call-update) | async-done | bytes 4194320 | tf_op jit(solution)/shard_map/all_gather | solution.py:133
  1716.6 64.2 %all-reduce.4.cloned.1.call-done = (bf16[1,1024,3,128]{3,1,2,0:T(8,128)(2,1)}, bf16[1,128,1024]{2,1,0:T(8,128)(2,1)}, bf16[1,1024,512]{2,1,0:T(8,128)(2,1)}, bf16[1,512,1024]{2,1,0:T(8,128)(2,1)}) async-done(((bf16[1,1024,3,128]{3,1,2,0:T(8,128)(2,1)}, bf16[1,128,1024]{2,1,0:T(8,128)(2,1)}, bf16[1,1024,512]{2,1,0:T(8,128)(2,1)}, bf16[1,512,1024]{2,1,0:T(8,128)(2,1)}), (bf16[1,1024,3,128]{3,1,2,0:T(8,128)(2,1)}, ...) | async-done | bytes 3145744 | tf_op jit(solution)/shard_map/psum | solution.py:322
  1787.4 67.7 %all-gather.79.cloned.1.call-done = bf16[2048,1024]{1,0:T(8,128)(2,1)} async-done(((bf16[256,1024]{1,0:T(8,128)(2,1)}), bf16[2048,1024]{1,0:T(8,128)(2,1)}) %all-gather.79.cloned.1.call-update) | async-done | bytes 4194320 | tf_op jit(solution)/shard_map/all_gather | solution.py:133
  1860.4 25.4 %all-reduce = (bf16[1,2,128]{2,1,0:T(2,128)(2,1)S(1)}, bf16[1,1024]{1,0:T(2,128)(2,1)S(1)}, bf16[1,512]{1,0:T(2,128)(2,1)S(1)}, bf16[1,1024]{1,0:T(2,128)(2,1)S(...) all-reduce(bf16[1,2,128]{2,1,0:T(2,128)(2,1)S(1)} %fusion.354, ...), channel_id=1, replica_groups=mesh['pipe'=2,'tensor'=8,'dp'=8] {'dp'}, use_global_device_ids=true, to_apply=%region_81.82 | all-reduce | flops 6912 | bytes 27648 | tf_op jit(solution)/shard_map/psum | solution.py:323
  (763 shorter events, 343.7 us)
Async XLA Ops:
  7.2 91.6 %copy-start = (bf16[1,512,1024]{2,1,0:T(8,128)(2,1)S(1)}, bf16[1,512,1024]{2,1,0:T(8,128)(2,1)}, u32[]{:S(2)}) copy-start(bf16[1,512,1024]{2,1,0:T(8,128)(2,1)} %param.21) | copy-start | bytes 3145732
  7.2 83.8 %all-gather.41.cloned.1.call-start = ((), (), s32[]{:S(2)}) async-start(), calls=%async_computation | async-start | bytes 4718592 | tf_op jit(solution)/shard_map/all_gather | solution.py:133
  11.5 696.5 %copy-start.166 = (f32[1,1,1024]{2,1,0:T(1,128)}, f32[1,1,1024]{2,1,0:T(1,128)S(1)}, u32[]{:S(2)}) copy-start(f32[1,1,1024]{2,1,0:T(1,128)S(1)} %get-tuple-element.102) | copy-start | bytes 12292
  16.9 152.9 %all-gather.43.cloned.1.call-start = ((), (), s32[]{:S(2)}) async-start(), calls=%async_computation.1 | async-start | bytes 4718592 | tf_op jit(solution)/shard_map/all_gather | solution.py:133
  100.2 163.9 %all-gather.45.cloned.1.call-start = ((), (), s32[]{:S(2)}) async-start(), calls=%async_computation.2 | async-start | bytes 4718592 | tf_op jit(solution)/shard_map/all_gather | solution.py:133
  174.3 13.3 collective-permute-start
  192.5 147.5 %all-gather.47.cloned.1.call-start = ((), (), s32[]{:S(2)}) async-start(), calls=%async_computation.3 | async-start | bytes 4718592 | tf_op jit(solution)/shard_map/all_gather | solution.py:133
  270.4 166.0 %all-gather.49.cloned.1.call-start = ((), (), s32[]{:S(2)}) async-start(), calls=%async_computation.4 | async-start | bytes 4718592 | tf_op jit(solution)/shard_map/all_gather | solution.py:133
  346.5 13.1 collective-permute-start.1
  364.9 150.6 %all-gather.51.cloned.1.call-start = ((), (), s32[]{:S(2)}) async-start(), calls=%async_computation.5 | async-start | bytes 4718592 | tf_op jit(solution)/shard_map/all_gather | solution.py:133
  445.9 164.1 %all-gather.53.cloned.1.call-start = ((), (), s32[]{:S(2)}) async-start(), calls=%async_computation.6 | async-start | bytes 4718592 | tf_op jit(solution)/shard_map/all_gather | solution.py:133
  521.0 12.3 collective-permute-start.2
  538.7 148.2 %all-gather.55.cloned.1.call-start = ((), (), s32[]{:S(2)}) async-start(), calls=%async_computation.7 | async-start | bytes 4718592 | tf_op jit(solution)/shard_map/all_gather | solution.py:133
  617.3 166.1 %all-gather.57.cloned.1.call-start = ((), (), s32[]{:S(2)}) async-start(), calls=%async_computation.8 | async-start | bytes 4718592 | tf_op jit(solution)/shard_map/all_gather | solution.py:133
  693.4 13.1 collective-permute-start.3
  711.8 152.9 %all-gather.61.cloned.1.call-start = ((), (), s32[]{:S(2)}) async-start(), calls=%async_computation.10 | async-start | bytes 4718592 | tf_op jit(solution)/shard_map/all_gather | solution.py:133
  788.7 82.5 %copy-start.144 = (f32[256]{0:T(256)}, f32[256]{0:T(256)S(1)}, u32[]{:S(2)}) copy-start(f32[256]{0:T(256)S(1)} %broadcast_multiply_fusion.20) | copy-start | bytes 3076
  795.2 162.9 %all-gather.63.cloned.1.call-start = ((), (), s32[]{:S(2)}) async-start(), calls=%async_computation.11 | async-start | bytes 4718592 | tf_op jit(solution)/shard_map/all_gather | solution.py:133
  888.4 166.2 %all-gather.65.cloned.1.call-start = ((), (), s32[]{:S(2)}) async-start(), calls=%async_computation.12 | async-start | bytes 4718592 | tf_op jit(solution)/shard_map/all_gather | solution.py:133
  966.3 15.2 collective-permute-start.4
  985.7 165.7 %all-gather.67.cloned.1.call-start = ((), (), s32[]{:S(2)}) async-start(), calls=%async_computation.13 | async-start | bytes 4718592 | tf_op jit(solution)/shard_map/all_gather | solution.py:133
  1081.8 167.9 %all-gather.69.cloned.1.call-start = ((), (), s32[]{:S(2)}) async-start(), calls=%async_computation.14 | async-start | bytes 4718592 | tf_op jit(solution)/shard_map/all_gather | solution.py:133
  1160.4 15.1 collective-permute-start.5
  1180.6 165.8 %all-gather.71.cloned.1.call-start = ((), (), s32[]{:S(2)}) async-start(), calls=%async_computation.15 | async-start | bytes 4718592 | tf_op jit(solution)/shard_map/all_gather | solution.py:133
  1276.9 167.8 %all-gather.73.cloned.1.call-start = ((), (), s32[]{:S(2)}) async-start(), calls=%async_computation.16 | async-start | bytes 4718592 | tf_op jit(solution)/shard_map/all_gather | solution.py:133
  1355.4 15.1 collective-permute-start.6
  1375.7 165.7 %all-gather.75.cloned.1.call-start = ((), (), s32[]{:S(2)}) async-start(), calls=%async_computation.17 | async-start | bytes 4718592 | tf_op jit(solution)/shard_map/all_gather | solution.py:133
  1471.7 166.2 %all-gather.77.cloned.1.call-start = ((), (), s32[]{:S(2)}) async-start(), calls=%async_computation.18 | async-start | bytes 4718592 | tf_op jit(solution)/shard_map/all_gather | solution.py:133
  1550.3 15.3 collective-permute-start.7
  1568.9 140.8 %all-gather.59.cloned.1.call-start = ((), (), s32[]{:S(2)}) async-start(), calls=%async_computation.9 | async-start | bytes 4718592 | tf_op jit(solution)/shard_map/all_gather | solution.py:133
  1576.5 204.4 %all-reduce.4.cloned.1.call-start = ((), (), s32[]{:S(2)}) async-start(), calls=%async_computation.20 | async-start | bytes 6291456 | tf_op jit(solution)/shard_map/psum | solution.py:322
  1663.3 191.8 %all-gather.79.cloned.1.call-start = ((), (), s32[]{:S(2)}) async-start(), calls=%async_computation.19 | async-start | bytes 4718592 | tf_op jit(solution)/shard_map/all_gather | solution.py:133
  (220 other events, 1903.8 us)
Sparse Core Ops, SparseCore 0:
  17.0 73.9 all-gather.40
  100.3 69.4 all-gather.42
  192.6 71.3 all-gather.44
  270.5 69.4 all-gather.46
  365.1 71.3 all-gather.48
  446.0 69.4 all-gather.50
  538.8 71.1 all-gather.52
  617.4 69.4 all-gather.54
  712.0 71.3 all-gather.56
  795.3 69.4 all-gather.60
  888.6 69.4 all-gather.62
  985.8 68.8 all-gather.64
  1081.9 69.4 all-gather.66
  1180.7 68.8 all-gather.68
  1277.0 69.4 all-gather.70
  1375.8 68.8 all-gather.72
  1471.9 69.4 all-gather.74
  1569.0 68.8 all-gather.76
  1640.2 69.4 all-gather.58
  1713.3 67.4 all-reduce.3
  1783.8 71.3 all-gather.78
